TPU v7x, 1024 devices: a whole 8x8x8 slice. The times are simulated.
1024 devices in a mesh: atom: 32 (over x, z_hi), energy: 32 (over z_lo, y, core).
Axes of the slice: x: 8, y: 8, z: 8 (z_hi: 4, z_lo: 2; z = z_hi * 2 + z_lo), core: 2. Of those that a mesh axis runs over, the one named last changes fastest.
Arguments:
- bare_green: bfloat16 [2, 12, 12, 128, 4096], P(None, None, None, 'atom', 'energy'), may hold values from -6 to 6
- coupling_grad: bfloat16 [8, 12, 12, 128], P(None, None, None, 'atom'), may hold values from -1.75 to 1.75
- neighbours: int32 [128, 8], P('atom'), may hold values from 0 to 127, as said below
- shifts: int32 [32], replicated, may hold values from 1 to 4
- strength: float32 [32], replicated, may hold values from 5e-05 to 0.0005
- occupation: float32 [32], replicated, may hold values from 0.1 to 4
Outputs:
- green: bfloat16 [2, 12, 12, 128, 4096], P(None, None, None, 'atom', 'energy')
Inputs may be any that keep to these rules, and one draw needn't show every extreme that they name: Each atom's 8 neighbours differ from it by 1 to 4 in index (not necessarily distinct); in every row one lies exactly 4 away.
All inputs are finite; a program needn't handle non-finite values.
Results may differ from a plain program's by a relative error of at most 0.0071.
Values may be sent and summed in bfloat16 or wider, within the bound.
A program may use at most 32 MiB of HBM per device.

v0:
```python
import jax
import jax.numpy as jnp
from jax import lax
from jax.sharding import PartitionSpec as P

WIDTH = 4


def padded(block, sides, width):
    for axis, dim in sides:
        count = lax.axis_size(axis)
        forward = [(i, i + 1) for i in range(count - 1)]
        backward = [(target, source) for source, target in forward]
        low = lax.ppermute(
            lax.slice_in_dim(block, block.shape[dim] - width, None, axis=dim), axis, forward
        )
        high = lax.ppermute(lax.slice_in_dim(block, 0, width, axis=dim), axis, backward)
        block = jnp.concatenate([low, block, high], axis=dim)
    return block


def coefficients(shifts, strength, occupation):
    offsets = jnp.arange(2 * WIDTH + 1, dtype=jnp.int32) - WIDTH
    lower_hit = offsets[:, None] == -shifts[None, :]
    upper_hit = offsets[:, None] == shifts[None, :]
    weights = jnp.where(lower_hit, (strength * occupation)[None, :], jnp.zeros((), jnp.float32))
    weights = weights + jnp.where(
        upper_hit, (strength * (occupation + 1.0))[None, :], jnp.zeros((), jnp.float32)
    )
    return jnp.sum(weights, axis=1).astype(jnp.bfloat16)


def band_matrix(offset_weights, energy_count):
    row_index = jnp.arange(energy_count + 2 * WIDTH, dtype=jnp.int32)[:, None]
    col_index = jnp.arange(energy_count, dtype=jnp.int32)[None, :]
    gap_index = row_index - col_index - WIDTH
    offsets = jnp.arange(2 * WIDTH + 1, dtype=jnp.int32) - WIDTH
    pick_mask = gap_index[None, :, :] == offsets[:, None, None]
    table = jnp.where(
        pick_mask, offset_weights.astype(jnp.float32)[:, None, None], jnp.zeros((), jnp.float32)
    )
    return jnp.sum(table, axis=0).astype(jnp.bfloat16)


def complex_product(factor_left, factor_right):
    real_part = jnp.einsum(
        "ikae,kjae->ijae", factor_left[0], factor_right[0], preferred_element_type=jnp.float32
    )
    real_part = real_part - jnp.einsum(
        "ikae,kjae->ijae", factor_left[1], factor_right[1], preferred_element_type=jnp.float32
    )
    imag_part = jnp.einsum(
        "ikae,kjae->ijae", factor_left[0], factor_right[1], preferred_element_type=jnp.float32
    )
    imag_part = imag_part + jnp.einsum(
        "ikae,kjae->ijae", factor_left[1], factor_right[0], preferred_element_type=jnp.float32
    )
    return jnp.stack([real_part, imag_part])


def convolve(extended, band_table):
    energy_count = band_table.shape[1]
    flat_rows = extended.reshape(-1, extended.shape[4])
    summed = jnp.dot(flat_rows, band_table, preferred_element_type=jnp.float32).astype(jnp.bfloat16)
    return summed.reshape(
        extended.shape[0], extended.shape[1], extended.shape[2], extended.shape[3], energy_count
    )


def sandwich(phonon_sum, index_row, grad_atom):
    picked = jnp.take(phonon_sum, index_row, axis=3)
    half_product = jnp.einsum(
        "nik,rklne->rilne", grad_atom, picked, preferred_element_type=jnp.float32
    ).astype(jnp.bfloat16)
    return jnp.einsum(
        "rilne,njl->rije", half_product, grad_atom, preferred_element_type=jnp.float32
    )


def per_device(bare_green, coupling_grad, neighbours, shifts, strength, occupation):
    atoms_here = bare_green.shape[3]
    energies_here = bare_green.shape[4]
    offset_weights = coefficients(shifts, strength, occupation)
    band_table = band_matrix(offset_weights, energies_here)
    local_index = neighbours - lax.axis_index("atom") * atoms_here + WIDTH
    bond_grads = jnp.moveaxis(coupling_grad, 3, 0)
    green_now = bare_green
    tall_block = padded(green_now, (("energy", 4),), WIDTH)
    narrow = convolve(tall_block, band_table)
    phonon_sum = padded(narrow, (("atom", 3),), WIDTH)

    def per_atom(atom_item):
        return sandwich(phonon_sum, atom_item[0], atom_item[1])

    self_energy = lax.map(per_atom, (local_index, bond_grads))
    self_energy = jnp.moveaxis(self_energy, 0, 3).astype(jnp.bfloat16)
    left_product = complex_product(bare_green, self_energy).astype(jnp.bfloat16)
    green_now = (bare_green.astype(jnp.float32) + complex_product(left_product, bare_green)).astype(
        jnp.bfloat16
    )
    return green_now


def solution(mesh):
    placed = (
        P(None, None, None, "atom", "energy"),
        P(None, None, None, "atom"),
        P("atom", None),
        P(),
        P(),
        P(),
    )
    return jax.shard_map(
        per_device,
        mesh=mesh,
        in_specs=placed,
        out_specs=P(None, None, None, "atom", "energy"),
        check_vma=False,
    )
```

profile of v0, /device:TPU:57, one launch (start us, length us, event | category | flops | bytes accessed | tf_op | source)
XLA Modules:
  0.0 108.1 jit_solution(13434567059049912215)
XLA Ops:
  0.0 1.3 %fusion.31 = (bf16[2,12,12,4,4]{4,3,2,1,0:T(4,128)(2,1)S(1)}, bf16[2,12,12,4,4]{4,3,2,1,0:T(4,128)(2,1)S(1)}) fusion(bf16[2,12,12,4,128]{4,3,2,1,0:T(4,128)(2,1)} %param.8), kind=kLoop, calls=%fused_computation.58 | loop fusion | bytes 36864 | tf_op jit(solution)/shard_map/slice | solution.py:15
  1.3 5.1 %collective-permute-start = (bf16[2,12,12,4,4]{4,3,2,1,0:T(4,128)(2,1)S(1)}, bf16[2,12,12,4,4]{4,3,2,1,0:T(4,128)(2,1)S(1)}, u32[]{:S(2)}, u32[]{:S(2)}) collective-permute-start(bf16[2,12,12,4,4]{4,3,2,1,0:T(4,128)(2,1)S(1)} %get-tuple-element.45), channel_id=1, source_target_pairs={{0,1},{1,2},{2,3},{3,4},{4,5},{5,6},{6,7},{7,8},{8,9},{9,10},{10,1... | collective-permute-start | bytes 27656 | tf_op jit(solution)/shard_map/ppermute | solution.py:14
  6.4 1.9 %collective-permute-start.1 = (bf16[2,12,12,4,4]{4,3,2,1,0:T(4,128)(2,1)S(1)}, bf16[2,12,12,4,4]{4,3,2,1,0:T(4,128)(2,1)S(1)}, u32[]{:S(2)}, u32[]{:S(2)}) collective-permute-start(bf16[2,12,12,4,4]{4,3,2,1,0:T(4,128)(2,1)S(1)} %get-tuple-element.46), channel_id=1, source_target_pairs={{1,0},{2,1},{3,2},{4,3},{5,4},{6,5},{7,6},{8,7},{9,8},{10,9},{11,1... | collective-permute-start | bytes 27656 | tf_op jit(solution)/shard_map/ppermute | solution.py:17
  10.7 4.9 %collective-permute-done.1 = bf16[2,12,12,4,4]{4,3,2,1,0:T(4,128)(2,1)S(1)} collective-permute-done((bf16[2,12,12,4,4]{4,3,2,1,0:T(4,128)(2,1)S(1)}, bf16[2,12,12,4,4]{4,3,2,1,0:T(4,128)(2,1)S(1)}, u32[]{:S(2)}, u32[]{:S(2)}) %collective-permute-start.1) | collective-permute-done | bytes 9248 | tf_op jit(solution)/shard_map/ppermute | solution.py:17
  15.7 1.8 %pad_maximum_fusion.1 = bf16[2,12,12,4,136]{4,3,2,1,0:T(4,128)(2,1)S(1)} fusion(bf16[2,12,12,4,4]{4,3,2,1,0:T(4,128)(2,1)S(1)} %collective-permute-done.1, bf16[2,12,12,4,128]{4,3,2,1,0:T(4,128)(2,1)} %param.8, bf16[2,12,12,4,4]{4,3,2,1,0:T(4,128)(2,1)S(1)} %collective-permute-done), kind=kLoop, calls=%fused_computation.46 | loop fusion | flops 940032 | bytes 626688 | tf_op jit(solution)/shard_map/concatenate | solution.py:18
  18.6 16.1 %collective-permute-start.3 = (bf16[2,12,12,4,128]{4,0,3,2,1:T(2,128)(2,1)S(1)}, bf16[2,12,12,4,128]{4,0,3,2,1:T(2,128)(2,1)}, u32[]{:S(2)}, u32[]{:S(2)}) collective-permute-start(bf16[2,12,12,4,128]{4,0,3,2,1:T(2,128)(2,1)S(1)} %copy.48), channel_id=1, source_target_pairs={{32,0},{64,32},{96,64},{128,96},{160,128},{192,160},{224,192},{256... | collective-permute-start | bytes 884744 | tf_op jit(solution)/shard_map/ppermute | solution.py:17
  34.7 2.1 %collective-permute-start.2 = (bf16[2,12,12,4,128]{4,0,3,2,1:T(2,128)(2,1)S(1)}, bf16[2,12,12,4,128]{4,0,3,2,1:T(2,128)(2,1)}, u32[]{:S(2)}, u32[]{:S(2)}) collective-permute-start(bf16[2,12,12,4,128]{4,0,3,2,1:T(2,128)(2,1)S(1)} %copy.48), channel_id=1, source_target_pairs={{0,32},{32,64},{64,96},{96,128},{128,160},{160,192},{192,224},{224... | collective-permute-start | bytes 884744 | tf_op jit(solution)/shard_map/ppermute | solution.py:14
  37.0 1.9 %copy.68 = bf16[1,12,12,4,128]{2,1,4,3,0:T(8,128)(2,1)S(1)} copy(bf16[1,12,12,4,128]{4,3,2,1,0:T(4,128)(2,1)S(1)} %get-tuple-element.43) | data formatting | bytes 294912
  38.9 2.6 %copy.67 = bf16[1,12,12,4,128]{2,1,4,3,0:T(8,128)(2,1)} copy(bf16[1,12,12,4,128]{4,3,2,1,0:T(4,128)(2,1)S(1)} %get-tuple-element.44) | data formatting | bytes 294912
  41.5 10.8 %collective-permute-done.2 = bf16[2,12,12,4,128]{4,0,3,2,1:T(2,128)(2,1)} collective-permute-done((bf16[2,12,12,4,128]{4,0,3,2,1:T(2,128)(2,1)S(1)}, bf16[2,12,12,4,128]{4,0,3,2,1:T(2,128)(2,1)}, u32[]{:S(2)}, u32[]{:S(2)}) %collective-permute-start.2) | collective-permute-done | bytes 294944 | tf_op jit(solution)/shard_map/ppermute | solution.py:14
  52.3 3.0 %pad_maximum_fusion = bf16[2,12,12,12,128]{4,0,3,2,1:T(2,128)(2,1)} fusion(bf16[2,12,12,4,128]{4,0,3,2,1:T(2,128)(2,1)} %collective-permute-done.3, bf16[2,12,12,4,128]{4,0,3,2,1:T(2,128)(2,1)S(1)} %copy.48, bf16[2,12,12,4,128]{4,0,3,2,1:T(2,128)(2,1)} %collective-permute-done.2), kind=kLoop, calls=%fused_computation.44 | loop fusion | flops 884736 | bytes 1769472 | tf_op jit(solution)/shard_map/concatenate | solution.py:18
  55.3 20.1 %while.10 = (s32[]{:T(128)}, bf16[4,2,12,12,128]{4,3,2,1,0:T(8,128)(2,1)S(1)}, bf16[4,8,12,12]{3,2,1,0:T(8,128)(2,1)S(1)}, s32[4,8]{1,0:T(4,128)S(1)}, bf16[2,12,12,12,128]{4,0,3,2,1:T(2,128)(2,1)}, /*index=5*/s32[]{:T(128)}) while((s32[]{:T(128)}, bf16[4,2,12,12,128]{4,3,2,1,0:T(8,128)(2,1)S(1)}, bf16[4,8,12,12]{3,2,1,0:T(8,128)(2,1)S(1)}, ...), condition=%wide.region_3.4_spmd, body=%wide.region_2.3_spmd.sunk | while | flops 14746698 | bytes 4592905 | solution.py:95
  55.3 3.3 %gather_fusion = bf16[8,2,12,12,128]{4,1,3,2,0:T(2,128)(2,1)S(1)} fusion(bf16[2,12,12,12,128]{4,0,3,2,1:T(2,128)(2,1)} %get-tuple-element.96, s32[1024]{0:T(1024)S(1)} %pad_clamp_fusion.2), kind=kCustom, calls=%fused_computation.clone.1 | custom fusion | bytes 1179680 | tf_op jit(solution)/shard_map/while/body/eval_jaxpr/jit(_take)/gather | solution.py:71
  60.4 3.3 %gather_fusion = bf16[8,2,12,12,128]{4,1,3,2,0:T(2,128)(2,1)S(1)} fusion(bf16[2,12,12,12,128]{4,0,3,2,1:T(2,128)(2,1)} %get-tuple-element.96, s32[1024]{0:T(1024)S(1)} %pad_clamp_fusion.2), kind=kCustom, calls=%fused_computation.clone.1 | custom fusion | bytes 1179680 | tf_op jit(solution)/shard_map/while/body/eval_jaxpr/jit(_take)/gather | solution.py:71
  65.4 3.3 %gather_fusion = bf16[8,2,12,12,128]{4,1,3,2,0:T(2,128)(2,1)S(1)} fusion(bf16[2,12,12,12,128]{4,0,3,2,1:T(2,128)(2,1)} %get-tuple-element.96, s32[1024]{0:T(1024)S(1)} %pad_clamp_fusion.2), kind=kCustom, calls=%fused_computation.clone.1 | custom fusion | bytes 1179680 | tf_op jit(solution)/shard_map/while/body/eval_jaxpr/jit(_take)/gather | solution.py:71
  70.4 3.3 %gather_fusion = bf16[8,2,12,12,128]{4,1,3,2,0:T(2,128)(2,1)S(1)} fusion(bf16[2,12,12,12,128]{4,0,3,2,1:T(2,128)(2,1)} %get-tuple-element.96, s32[1024]{0:T(1024)S(1)} %pad_clamp_fusion.2), kind=kCustom, calls=%fused_computation.clone.1 | custom fusion | bytes 1179680 | tf_op jit(solution)/shard_map/while/body/eval_jaxpr/jit(_take)/gather | solution.py:71
  75.4 4.4 %copy.51 = bf16[4,2,12,12,128]{2,3,4,0,1:T(8,128)(2,1)} copy(bf16[4,2,12,12,128]{4,3,2,1,0:T(8,128)(2,1)S(1)} %get-tuple-element.32) | data formatting | bytes 589824 | tf_op jit(solution)/shard_map/convert_element_type | solution.py:96
  79.8 3.6 %fusion.23 = f32[4,128,12,12]{3,2,1,0:T(8,128)S(1)} fusion(bf16[1,12,12,4,128]{2,1,4,3,0:T(8,128)(2,1)} %copy.67, bf16[2,12,12,4,128]{1,2,4,3,0:T(8,128)(2,1)} %bitcast.97), kind=kOutput, calls=%fused_computation.39 | convolution fusion | flops 1769472 | bytes 4489216 | tf_op jit(solution)/shard_map/ikae,kjae->ijae/dot_general | solution.py:52
  87.3 2.5 %fusion.16 = f32[4,128,12,12]{3,2,1,0:T(8,128)} fusion(bf16[4,128,12,12]{3,2,1,0:T(8,128)(2,1)S(1)} %subtract_convert_fusion, bf16[1,12,12,4,128]{2,1,4,3,0:T(8,128)(2,1)S(1)} %copy-done), kind=kOutput, calls=%fused_computation.32 | convolution fusion | flops 1769472 | bytes 589824 | tf_op jit(solution)/shard_map/ikae,kjae->ijae/dot_general | solution.py:46
  91.1 1.4 %copy-done.2 = bf16[4,128,12,12]{3,2,1,0:T(8,128)(2,1)} copy-done((bf16[4,128,12,12]{3,2,1,0:T(8,128)(2,1)}, bf16[4,128,12,12]{3,2,1,0:T(8,128)(2,1)S(1)}, u32[]{:S(2)}) %copy-start.2) | copy-done | bytes 147480
  92.4 2.5 %add_bitcast_fusion = f32[1,12,12,4,128]{2,1,4,3,0:T(8,128)} fusion(f32[4,128,12,12]{3,2,1,0:T(8,128)S(1)} %fusion.14, bf16[4,128,12,12]{3,2,1,0:T(8,128)(2,1)S(1)} %add_convert_fusion, bf16[1,12,12,4,128]{2,1,4,3,0:T(8,128)(2,1)S(1)} %copy-done), kind=kOutput, calls=%fused_computation.21 | convolution fusion | flops 1843200 | bytes 884736 | tf_op jit(solution)/shard_map/ikae,kjae->ijae/dot_general | solution.py:55
  94.9 3.3 %copy.59 = f32[1,12,12,4,128]{4,3,2,1,0:T(4,128)S(1)} copy(f32[1,12,12,4,128]{2,1,4,3,0:T(8,128)} %add_bitcast_fusion) | data formatting | bytes 589824 | tf_op jit(solution)/shard_map/stack | solution.py:58
  98.3 5.6 %subtract_bitcast_fusion = f32[1,12,12,4,128]{2,1,4,3,0:T(8,128)} fusion(f32[4,128,12,12]{3,2,1,0:T(8,128)} %fusion.16, bf16[4,128,12,12]{3,2,1,0:T(8,128)(2,1)} %copy-done.2, bf16[1,12,12,4,128]{2,1,4,3,0:T(8,128)(2,1)S(1)} %copy.68), kind=kOutput, calls=%fused_computation.22 | convolution fusion | flops 1843200 | bytes 884736 | tf_op jit(solution)/shard_map/ikae,kjae->ijae/dot_general | solution.py:49
  103.9 3.3 %copy.58 = f32[1,12,12,4,128]{4,3,2,1,0:T(4,128)S(1)} copy(f32[1,12,12,4,128]{2,1,4,3,0:T(8,128)} %subtract_bitcast_fusion) | data formatting | bytes 589824 | tf_op jit(solution)/shard_map/stack | solution.py:58
  (56 shorter events, 16.4 us)
Async XLA Ops:
  1.3 9.4 %collective-permute-start = (bf16[2,12,12,4,4]{4,3,2,1,0:T(4,128)(2,1)S(1)}, bf16[2,12,12,4,4]{4,3,2,1,0:T(4,128)(2,1)S(1)}, u32[]{:S(2)}, u32[]{:S(2)}) collective-permute-start(bf16[2,12,12,4,4]{4,3,2,1,0:T(4,128)(2,1)S(1)} %get-tuple-element.45), channel_id=1, source_target_pairs={{0,1},{1,2},{2,3},{3,4},{4,5},{5,6},{6,7},{7,8},{8,9},{9,10},{10,1... | collective-permute-start | bytes 27656 | tf_op jit(solution)/shard_map/ppermute | solution.py:14
  6.4 9.3 %collective-permute-start.1 = (bf16[2,12,12,4,4]{4,3,2,1,0:T(4,128)(2,1)S(1)}, bf16[2,12,12,4,4]{4,3,2,1,0:T(4,128)(2,1)S(1)}, u32[]{:S(2)}, u32[]{:S(2)}) collective-permute-start(bf16[2,12,12,4,4]{4,3,2,1,0:T(4,128)(2,1)S(1)} %get-tuple-element.46), channel_id=1, source_target_pairs={{1,0},{2,1},{3,2},{4,3},{5,4},{6,5},{7,6},{8,7},{9,8},{10,9},{11,1... | collective-permute-start | bytes 27656 | tf_op jit(solution)/shard_map/ppermute | solution.py:17
  10.7 26.1 %copy-start.3 = (bf16[2,12,12,4,128]{4,3,2,1,0:T(4,128)(2,1)S(1)}, bf16[2,12,12,4,128]{4,3,2,1,0:T(4,128)(2,1)}, u32[]{:S(2)}) copy-start(bf16[2,12,12,4,128]{4,3,2,1,0:T(4,128)(2,1)} %param.8) | copy-start | bytes 884740
  10.7 26.2 %copy-start.4 = (bf16[8,12,12,4]{2,3,1,0:T(4,128)(2,1)S(1)}, bf16[8,12,12,4]{2,3,1,0:T(4,128)(2,1)}, u32[]{:S(2)}) copy-start(bf16[8,12,12,4]{2,3,1,0:T(4,128)(2,1)} %param.9) | copy-start | bytes 27652
  18.6 22.9 %collective-permute-start.3 = (bf16[2,12,12,4,128]{4,0,3,2,1:T(2,128)(2,1)S(1)}, bf16[2,12,12,4,128]{4,0,3,2,1:T(2,128)(2,1)}, u32[]{:S(2)}, u32[]{:S(2)}) collective-permute-start(bf16[2,12,12,4,128]{4,0,3,2,1:T(2,128)(2,1)S(1)} %copy.48), channel_id=1, source_target_pairs={{32,0},{64,32},{96,64},{128,96},{160,128},{192,160},{224,192},{256... | collective-permute-start | bytes 884744 | tf_op jit(solution)/shard_map/ppermute | solution.py:17
  34.7 17.6 %collective-permute-start.2 = (bf16[2,12,12,4,128]{4,0,3,2,1:T(2,128)(2,1)S(1)}, bf16[2,12,12,4,128]{4,0,3,2,1:T(2,128)(2,1)}, u32[]{:S(2)}, u32[]{:S(2)}) collective-permute-start(bf16[2,12,12,4,128]{4,0,3,2,1:T(2,128)(2,1)S(1)} %copy.48), channel_id=1, source_target_pairs={{0,32},{32,64},{64,96},{96,128},{128,160},{160,192},{192,224},{224... | collective-permute-start | bytes 884744 | tf_op jit(solution)/shard_map/ppermute | solution.py:14
  37.0 4.5 %copy-start.5 = (s32[4,8]{1,0:T(4,128)S(1)}, s32[4,8]{1,0:T(4,128)}, u32[]{:S(2)}) copy-start(s32[4,8]{1,0:T(4,128)} %param.10) | copy-start | bytes 388
  79.8 3.6 %copy-start = (bf16[1,12,12,4,128]{2,1,4,3,0:T(8,128)(2,1)S(1)}, bf16[1,12,12,4,128]{2,1,4,3,0:T(8,128)(2,1)}, u32[]{:S(2)}) copy-start(bf16[1,12,12,4,128]{2,1,4,3,0:T(8,128)(2,1)} %copy.67) | copy-start | bytes 442372
  79.8 4.1 %copy-start.1 = (bf16[4,2,12,12,128]{2,3,4,0,1:T(8,128)(2,1)S(1)}, bf16[4,2,12,12,128]{2,3,4,0,1:T(8,128)(2,1)}, u32[]{:S(2)}) copy-start(bf16[4,2,12,12,128]{2,3,4,0,1:T(8,128)(2,1)} %copy.51) | copy-start | bytes 884740
  91.0 1.4 %copy-start.2 = (bf16[4,128,12,12]{3,2,1,0:T(8,128)(2,1)}, bf16[4,128,12,12]{3,2,1,0:T(8,128)(2,1)S(1)}, u32[]{:S(2)}) copy-start(bf16[4,128,12,12]{3,2,1,0:T(8,128)(2,1)S(1)} %add_convert_fusion) | copy-start | bytes 442372
where the time goes:
time: 109 us; the launch traced here: 108 us
  local copies, waits for them, and re-layouts  32.7 us (30%)
  starting transfers between devices  25.2 us (23%)
  matrix products  23.5 us (22%)
  waiting for transfers between devices  15.8 us (14%)
  other arithmetic  10.4 us (10%)
    ppermute x2, starting transfers between devices, padded(): lax.ppermute(lax.slice_in_dim(block, 0, width, axis=dim), axis, backward)  18 us
    gather x4, local copies, waits for them, and re-layouts, sandwich(): picked = jnp.take(phonon_sum, index_row, axis=3)  13.1 us
    ppermute x2, waiting for transfers between devices, padded(): lax.ppermute(lax.slice_in_dim(block, block.shape[dim] - width, None, axis...  10.8 us
    ppermute x2, starting transfers between devices, padded(): lax.ppermute(lax.slice_in_dim(block, block.shape[dim] - width, None, axis...  7.19 us
    dot_general x2, matrix products, complex_product(): jnp.einsum('ikae,kjae->ijae', factor_left[1], factor_right[1], preferred_...  6.89 us
    another operation x2, local copies, waits for them, and re-layouts, complex_product(): return jnp.stack([real_part, imag_part])  6.62 us
    unnamed x15, local copies, waits for them, and re-layouts  6.4 us
    ppermute x2, waiting for transfers between devices, padded(): lax.ppermute(lax.slice_in_dim(block, 0, width, axis=dim), axis, backward)  4.94 us
  transfers between devices with their start and end apart: 4, of which 2 were waited for; matrix products, arithmetic and copies ran while one was open for 6% of the time, Pallas kernels for 0%

commit v1 on v0

v1 whole, which is shorter than its diff:
```python
import functools

import jax
import jax.numpy as jnp
from jax import lax
from jax.experimental import pallas as pl
from jax.experimental.pallas import tpu as pltpu
from jax.sharding import PartitionSpec as P

WIDTH = 4
MESH = pl.DeviceIdType.MESH
F32 = jnp.float32
BF16 = jnp.bfloat16


def iota(shape, dim):
    return lax.broadcasted_iota(jnp.int32, shape, dim)


def offset_weight_rows(shifts, strength, occupation):
    row = iota((8, shifts.shape[1]), 0)
    size = jnp.where(row < WIDTH, WIDTH - row, row - (WIDTH - 1))
    extra = jnp.where(row < WIDTH, 0.0, 1.0).astype(F32)
    picked = jnp.where(size == shifts, strength * (occupation + extra), 0.0)
    return jnp.sum(picked, axis=1, keepdims=True).astype(BF16).astype(F32)


def band_from_gap(gap, weights):
    table = jnp.zeros(gap.shape, F32)
    for row in range(8):
        offset = row - WIDTH if row < WIDTH else row - WIDTH + 1
        table = jnp.where(gap == offset, weights[row : row + 1, 0:1], table)
    return table


def dot(left, right):
    return jnp.dot(left, right, preferred_element_type=F32)


def kernel(
    orb, bonds, atoms, atom_count, energy_count, chunks, raw,
    x_hbm, g_hbm, nb_hbm, sh_hbm, st_hbm, oc_hbm,
    out_ref,
    xv, gv, nbs, shv, stv, ocv,
    ebuf, halo, rim, rim_in, own, left, right,
    gf, ga, mbuf, wbuf, bf, bdup, sacc, sdup, tbuf,
    load_sem, edge_send, edge_recv, rim_send, rim_recv, slab_send, slab_recv,
):
    lanes = xv.shape[-1]
    inner = orb * atoms
    per = orb // chunks
    here_a = lax.axis_index("atom")
    here_e = lax.axis_index("energy")
    sides = ((here_a + 1, here_a < atom_count - 1), (here_a - 1, here_a > 0))
    energy_sides = ((here_e - 1, here_e > 0), (here_e + 1, here_e < energy_count - 1))

    loads = [
        pltpu.make_async_copy(src, dst, load_sem.at[slot])
        for slot, (src, dst) in enumerate(
            ((x_hbm, xv), (sh_hbm, shv), (st_hbm, stv), (oc_hbm, ocv), (g_hbm, gv), (nb_hbm, nbs))
        )
    ]
    for copy in loads:
        copy.start()
    barrier = pltpu.get_barrier_semaphore()
    expected = jnp.int32(0)
    for axis, group in (("atom", sides), ("energy", energy_sides)):
        for peer, exists in group:
            expected = expected + jnp.where(exists, 1, 0)

            @pl.when(exists)
            def _():
                pl.semaphore_signal(barrier, inc=1, device_id={axis: peer}, device_id_type=MESH)

    for side, (_, exists) in enumerate(energy_sides):

        @pl.when(jnp.logical_not(exists))
        def _():
            halo[side] = jnp.zeros(halo.shape[1:], BF16)

    for landing, (_, exists) in ((right, sides[0]), (left, sides[1])):

        @pl.when(jnp.logical_not(exists))
        def _():
            landing[...] = jnp.zeros_like(landing)

    for copy in loads[1:4]:
        copy.wait()
    weights = offset_weight_rows(shv[...], stv[...], ocv[...])
    band = band_from_gap(iota((lanes, lanes), 0) - iota((lanes, lanes), 1), weights).astype(BF16)
    edge_row, edge_col = iota((8, lanes), 0), iota((8, lanes), 1)
    edge_energy = jnp.where(edge_row < WIDTH, edge_row - WIDTH, edge_row - WIDTH + lanes)
    corner = band_from_gap(edge_energy - edge_col, weights).astype(BF16)

    loads[0].wait()
    raw_count = raw * per
    flat = [
        xv[:, :raw_count].reshape(2 * raw_count * inner, lanes),
        xv[:, raw_count:].reshape(2 * (orb - raw_count) * inner, lanes),
    ]
    split = flat[0].shape[0]
    pick_row, pick_col = iota((16, lanes), 0), iota((16, lanes), 1)
    target = jnp.where(pick_row < 8, pick_row - WIDTH, pick_row - 8 + lanes - WIDTH)
    pick = jnp.where((pick_col == target) & (pick_row >= WIDTH) & (pick_row < 12), 1.0, 0.0).astype(BF16)
    edges = [
        lax.dot_general(pick, part, (((1,), (1,)), ((), ())), preferred_element_type=F32).astype(BF16)
        for part in flat
    ]
    for side in range(2):
        ebuf[side, :, :split] = edges[0][side * 8 : side * 8 + 8]
        ebuf[side, :, split:] = edges[1][side * 8 : side * 8 + 8]

    pl.semaphore_wait(barrier, expected)

    def edge_copy(side):
        return pltpu.make_async_remote_copy(
            src_ref=ebuf.at[side], dst_ref=halo.at[1 - side],
            send_sem=edge_send.at[side], recv_sem=edge_recv.at[1 - side],
            device_id={"energy": energy_sides[side][0]}, device_id_type=MESH,
        )

    def slab_copy(side, chunk):
        span = pl.ds(chunk * per, per)
        landing = (left, right)[side]
        source = xv if isinstance(chunk, int) and chunk < raw else own
        return pltpu.make_async_remote_copy(
            src_ref=source.at[:, span], dst_ref=landing.at[:, span],
            send_sem=slab_send.at[side, chunk], recv_sem=slab_recv.at[side, chunk],
            device_id={"atom": sides[side][0]}, device_id_type=MESH,
        )

    def rim_copy(side):
        return pltpu.make_async_remote_copy(
            src_ref=rim, dst_ref=rim_in.at[side],
            send_sem=rim_send.at[side], recv_sem=rim_recv.at[side],
            device_id={"atom": sides[side][0]}, device_id_type=MESH,
        )

    def start_sends(make):
        for side in range(2):

            @pl.when(sides[side][1])
            def _():
                make(side).start()

    def wait_landed(make):
        for side in range(2):

            @pl.when(sides[1 - side][1])
            def _():
                make(side).wait_recv()

    def wait_sent(make):
        for side in range(2):

            @pl.when(sides[side][1])
            def _():
                make(side).wait_send()

    for side in range(2):

        @pl.when(energy_sides[side][1])
        def _():
            edge_copy(side).start()

    for chunk in range(raw):
        start_sends(functools.partial(slab_copy, chunk=chunk))

    def beyond(edge_values):
        return lax.dot_general(edge_values, corner, (((0,), (0,)), ((), ())), preferred_element_type=F32)

    inside = dot(flat[1], band)
    for side in range(2):

        @pl.when(energy_sides[1 - side][1])
        def _():
            edge_copy(side).wait_recv()

    both = halo[0] + halo[1]
    rim[...] = both[:, :split]
    start_sends(rim_copy)
    rest = (inside + beyond(both[:, split:])).astype(BF16)
    own[:, raw_count:] = rest.reshape(2, orb - raw_count, inner, lanes)
    for chunk in range(raw, chunks):
        start_sends(functools.partial(slab_copy, chunk=chunk))
    first_part = (dot(flat[0], band) + beyond(both[:, :split])).astype(BF16)
    own[:, :raw_count] = first_part.reshape(2, raw_count, inner, lanes)

    for copy in loads[4:]:
        copy.wait()
    gf[...] = gv[...].astype(F32)
    ga[...] = jnp.zeros_like(ga)
    for atom in range(atoms):
        picked = [
            gf[pl.ds(atoms * o + atom, bonds, stride=inner), :] for o in range(orb)
        ]
        ga[atom, :, 0:orb] = jnp.concatenate(picked, axis=0).astype(BF16)

    wide = 3 * inner
    source_row, source_col = iota((lanes, wide), 0), iota((lanes, wide), 1)
    spread = jnp.where(source_row == lax.rem(source_col, inner) // atoms, 1.0, 0.0).astype(BF16)
    bond_row, bond_col = iota((bonds, wide), 0), iota((bonds, wide), 1)
    local_id = (bond_col // inner) * atoms + lax.rem(bond_col, atoms)
    for atom in range(atoms):
        near = jnp.zeros((bonds, wide), jnp.int32)
        for bond in range(bonds):
            near = jnp.where(bond_row == bond, nbs[atom, bond], near)
        hit = (near - here_a * atoms + atoms) == local_id
        table = dot(ga[atom], spread).reshape(orb, bonds, wide)
        table = jnp.where(hit[None], table, 0.0).reshape(orb * bonds, wide)
        mbuf[atom * orb * bonds : (atom + 1) * orb * bonds, :] = table.astype(BF16)

    pairs = orb * orb
    span = per * orb * bonds
    lift = jnp.where(
        iota((pairs, orb * bonds), 0) // orb == iota((pairs, orb * bonds), 1) // bonds, 1.0, 0.0
    ).astype(BF16)
    same_bond = lax.rem(iota((orb * bonds, span), 0), bonds) == lax.rem(
        iota((orb * bonds, span), 1), bonds
    )
    same_orbital = lax.rem(iota((pairs, span), 0), orb) == lax.rem(
        iota((pairs, span), 1), orb * bonds
    ) // bonds
    which = iota((lanes, span), 1) // (orb * bonds)

    def build_w(step, carry):
        atom, chunk = step // chunks, lax.rem(step, chunks)
        spread_k = jnp.where(iota((lanes, span), 0) == chunk * per + which, 1.0, 0.0).astype(BF16)
        table = jnp.where(same_bond, dot(ga[atom], spread_k), 0.0).astype(BF16)
        wbuf[atom, chunk] = jnp.where(same_orbital, dot(lift, table), 0.0).astype(BF16)
        return carry

    lax.fori_loop(0, atoms * chunks, build_w, 0)

    tiles = inner // 8
    upper = iota((tiles, 8, lanes), 1) < atoms

    def build_b(o, carry):
        real = xv[0, o].astype(F32).reshape(tiles, 8, lanes)
        imag = xv[1, o].astype(F32).reshape(tiles, 8, lanes)
        for part, value in enumerate((real, imag, real + imag)):
            bf[part, o] = value
            turned = pltpu.roll(value, atoms, 1)
            bdup[part, o, :, 0] = jnp.where(upper, value, turned)
            bdup[part, o, :, 1] = jnp.where(upper, turned, value)
        return carry

    lax.fori_loop(0, orb, build_b, 0)

    for chunk in range(raw):
        wait_landed(functools.partial(slab_copy, chunk=chunk))
    wait_landed(rim_copy)
    for side, landing in enumerate((left, right)):

        @pl.when(sides[1 - side][1])
        def _():
            values = landing[:, :raw_count].reshape(split, lanes)
            sums = (dot(values, band) + beyond(rim_in[side])).astype(BF16)
            landing[:, :raw_count] = sums.reshape(2, raw_count, inner, lanes)

    def chunk_terms(chunk):
        halves = []
        for step in range(per):
            k = chunk * per + step
            stack = jnp.concatenate(
                [
                    jnp.concatenate([left[r, k], own[r, k], right[r, k]], axis=0)
                    for r in range(2)
                ],
                axis=1,
            )
            halves.append(dot(mbuf[...], stack).astype(BF16))
        size = orb * bonds
        return [
            dot(
                wbuf[atom, chunk],
                jnp.concatenate([half[atom * size : (atom + 1) * size] for half in halves], axis=0),
            )
            for atom in range(atoms)
        ]

    for atom, term in enumerate(chunk_terms(0)):
        sacc[atom] = term

    def middle(chunk, carry):
        for atom, term in enumerate(chunk_terms(chunk)):
            sacc[atom] += term
        return carry

    lax.fori_loop(1, raw, middle, 0)

    def landing_chunk(chunk, carry):
        wait_landed(functools.partial(slab_copy, chunk=chunk))
        return middle(chunk, carry)

    lax.fori_loop(raw, chunks - 1, landing_chunk, 0)
    wait_landed(functools.partial(slab_copy, chunk=chunks - 1))
    for atom, term in enumerate(chunk_terms(chunks - 1)):
        total = sacc[atom] + term
        real, imag = total[:, :lanes], total[:, lanes:]
        for part, value in enumerate((real, imag, real + imag)):
            for copy in range(2):
                sdup[part, pl.ds(atom + copy * atoms, pairs, stride=8), :] = value

    def products(factor, other, row):
        sums = [jnp.zeros((tiles, 8, lanes), F32) for _ in range(3)]
        for k in range(orb):
            for part in range(3):
                sums[part] = sums[part] + factor(part, row, k)[None] * other[part, k]
        real = sums[0] - sums[1]
        return real, sums[2] - sums[0] - sums[1]

    def from_sdup(part, row, k):
        return sdup[part, pl.ds(pl.multiple_of((row * orb + k) * 8, 8), 8), :]

    def from_bdup(part, row, k):
        return bdup[part, row, k // 2, k % 2]

    def first(row, carry):
        real, imag = products(from_sdup, bf, row)
        tbuf[0, row] = real
        tbuf[1, row] = imag
        tbuf[2, row] = real + imag
        return carry

    lax.fori_loop(0, orb, first, 0)

    def second(row, carry):
        for part, value in enumerate(products(from_bdup, tbuf, row)):
            total = (value + bf[part, row]).reshape(inner, lanes)
            out_ref[part, row] = total.astype(out_ref.dtype)
        return carry

    lax.fori_loop(0, orb, second, 0)

    for side in range(2):

        @pl.when(energy_sides[side][1])
        def _():
            edge_copy(side).wait_send()

    wait_sent(rim_copy)
    for chunk in range(chunks):
        wait_sent(functools.partial(slab_copy, chunk=chunk))


def per_device(atom_count, energy_count, chunks, raw, bare_green, coupling_grad, neighbours, shifts, strength, occupation):
    _, orb, _, atoms, lanes = bare_green.shape
    bonds = coupling_grad.shape[0]
    inner = orb * atoms
    waves = shifts.shape[0]
    x = bare_green.reshape(2, orb, inner, lanes)
    g = jnp.transpose(coupling_grad, (0, 1, 3, 2)).reshape(bonds * inner, orb)
    per = orb // chunks
    tiles = inner // 8
    any_spec = pl.BlockSpec(memory_space=pl.ANY)
    result = pl.pallas_call(
        functools.partial(kernel, orb, bonds, atoms, atom_count, energy_count, chunks, raw),
        out_shape=jax.ShapeDtypeStruct(x.shape, x.dtype),
        in_specs=[any_spec] * 6,
        out_specs=pl.BlockSpec(memory_space=pltpu.VMEM),
        scratch_shapes=[
            pltpu.VMEM(x.shape, BF16),
            pltpu.VMEM(g.shape, BF16),
            pltpu.SMEM(neighbours.shape, jnp.int32),
            pltpu.VMEM((1, waves), jnp.int32),
            pltpu.VMEM((1, waves), F32),
            pltpu.VMEM((1, waves), F32),
            pltpu.VMEM((2, 8, 2 * orb * inner), BF16),
            pltpu.VMEM((2, 8, 2 * orb * inner), BF16),
            pltpu.VMEM((8, 2 * raw * per * inner), BF16),
            pltpu.VMEM((2, 8, 2 * raw * per * inner), BF16),
            pltpu.VMEM(x.shape, BF16),
            pltpu.VMEM(x.shape, BF16),
            pltpu.VMEM(x.shape, BF16),
            pltpu.VMEM(g.shape, F32),
            pltpu.VMEM((atoms, orb * bonds, lanes), BF16),
            pltpu.VMEM((atoms * orb * bonds, 3 * inner), BF16),
            pltpu.VMEM((atoms, chunks, orb * orb, per * orb * bonds), BF16),
            pltpu.VMEM((3, orb, tiles, 8, lanes), F32),
            pltpu.VMEM((3, orb, tiles, 2, 8, lanes), F32),
            pltpu.VMEM((atoms, orb * orb, 2 * lanes), F32),
            pltpu.VMEM((3, orb * orb * 8, lanes), F32),
            pltpu.VMEM((3, orb, tiles, 8, lanes), F32),
            pltpu.SemaphoreType.DMA((6,)),
            pltpu.SemaphoreType.DMA((2,)),
            pltpu.SemaphoreType.DMA((2,)),
            pltpu.SemaphoreType.DMA((2,)),
            pltpu.SemaphoreType.DMA((2,)),
            pltpu.SemaphoreType.DMA((2, chunks)),
            pltpu.SemaphoreType.DMA((2, chunks)),
        ],
        compiler_params=pltpu.CompilerParams(collective_id=0, has_side_effects=True),
    )(x, g, neighbours, shifts.reshape(1, waves), strength.reshape(1, waves), occupation.reshape(1, waves))
    return result.reshape(bare_green.shape)


def solution(mesh):
    placed = (
        P(None, None, None, "atom", "energy"),
        P(None, None, None, "atom"),
        P("atom", None),
        P(),
        P(),
        P(),
    )
    body = functools.partial(per_device, mesh.shape["atom"], mesh.shape["energy"], 6, 2)
    return jax.shard_map(
        body,
        mesh=mesh,
        in_specs=placed,
        out_specs=P(None, None, None, "atom", "energy"),
        check_vma=False,
    )
```

time: 109 us -> 37.8 us (0.35)
  the two profiles are of different devices: /device:TPU:57 before, /device:TPU:63 now
where the time goes in v1:
time: 37.8 us; the launch traced here: 37.6 us
  Pallas kernels  35.8 us (95%)
  local copies, waits for them, and re-layouts  1.78 us (5%)
    pallas_call x1, Pallas kernels, per_device(): pl.pallas_call(functools.partial(kernel, orb, bonds, atoms, atom_count, e...  35.8 us
    unnamed x1, local copies, waits for them, and re-layouts  1.78 us

profile of v1, /device:TPU:63, one launch (start us, length us, event | category | flops | bytes accessed | tf_op | source)
XLA Modules:
  0.0 37.6 jit_solution(11089210946153497488)
XLA Ops:
  0.0 35.8 %shard_map.64 = bf16[2,12,48,128]{3,2,1,0:T(8,128)(2,1)} custom-call(bf16[2,12,48,128]{3,2,1,0:T(8,128)(2,1)} %bitcast.9, bf16[384,12]{1,0:T(8,128)(2,1)} %bitcast.10, s32[4,8]{1,0:T(4,128)} %nb_hbm.1, s32[1,32]{1,0:T(1,128)} %bitcast.11, f32[1,32]{1,0:T(1,128)} %bitcast.12, f32[1,32]{1,0:T(1,128)} %bitcast.13), custom_call_target="tpu_custom_call" | custom-call | tf_op jit(solution)/shard_map/pallas_call | solution.py:357
  35.8 1.8 %copy.8 = bf16[2,12,12,4,128]{4,3,2,1,0:T(4,128)(2,1)} copy(bf16[2,12,12,4,128]{4,3,2,1,0:T(4,128)(2,1)} %bitcast.8) | data formatting | bytes 589824

commit v2 on v0

v2 whole, which is shorter than its diff:
```python
import functools

import jax
import jax.numpy as jnp
from jax import lax
from jax.experimental import pallas as pl
from jax.experimental.pallas import tpu as pltpu
from jax.sharding import PartitionSpec as P

WIDTH = 4
GROUP = 4
MESH = pl.DeviceIdType.MESH
F32 = jnp.float32
BF16 = jnp.bfloat16


def iota(shape, dim):
    return lax.broadcasted_iota(jnp.int32, shape, dim)


def offset_weight_rows(shifts, strength, occupation):
    row = iota((8, shifts.shape[1]), 0)
    size = jnp.where(row < WIDTH, WIDTH - row, row - (WIDTH - 1))
    extra = jnp.where(row < WIDTH, 0.0, 1.0).astype(F32)
    picked = jnp.where(size == shifts, strength * (occupation + extra), 0.0)
    return jnp.sum(picked, axis=1, keepdims=True).astype(BF16).astype(F32)


def band_from_gap(gap, weights):
    table = jnp.zeros(gap.shape, F32)
    for row in range(8):
        offset = row - WIDTH if row < WIDTH else row - WIDTH + 1
        table = jnp.where(gap == offset, weights[row : row + 1, 0:1], table)
    return table


def dot(left, right):
    return jnp.dot(left, right, preferred_element_type=F32)


def kernel(
    orb, bonds, atoms, atom_count, energy_count, raw,
    x_hbm, g_hbm, nb_hbm, sh_hbm, st_hbm, oc_hbm,
    out_ref,
    xv, gv, nbs, shv, stv, ocv,
    x32, xs, ebuf, halo, rim, rim_in, own, left, right,
    gf, gz, ga, e1, kbuf, bpad, sacc, se, tbuf, out32,
    ready, answer, load_sem, edge_send, edge_recv, rim_send, rim_recv, slab_send, slab_recv,
):
    lanes = xv.shape[-1]
    inner = orb * atoms
    pairs = orb * orb
    high = gz.shape[2]
    here_a = lax.axis_index("atom")
    here_e = lax.axis_index("energy")
    sides = ((here_a + 1, here_a < atom_count - 1), (here_a - 1, here_a > 0))
    energy_sides = ((here_e - 1, here_e > 0), (here_e + 1, here_e < energy_count - 1))

    loads = [
        pltpu.make_async_copy(src, dst, load_sem.at[slot])
        for slot, (src, dst) in enumerate(
            ((x_hbm, xv), (sh_hbm, shv), (st_hbm, stv), (oc_hbm, ocv), (g_hbm, gv), (nb_hbm, nbs))
        )
    ]
    for copy in loads:
        copy.start()
    barrier = pltpu.get_barrier_semaphore()
    expected = jnp.int32(0)
    role = lax.rem(here_a, GROUP)
    heard = (sides[0][1] & (role == GROUP - 1), sides[1][1] & (role != 0))
    answered = (sides[0][1] & (role != GROUP - 1), sides[1][1] & (role == 0))
    for axis, peer, exists in (
        ("atom", sides[0][0], answered[0]),
        ("atom", sides[1][0], answered[1]),
        ("energy", *energy_sides[1]),
        ("energy", energy_sides[0][0], here_e == 1),
    ):

        @pl.when(exists)
        def _():
            pl.semaphore_signal(barrier, inc=1, device_id={axis: peer}, device_id_type=MESH)

    for exists in (heard[0], heard[1], energy_sides[0][1], here_e == 0):
        expected = expected + jnp.where(exists, 1, 0)

    def edge_copy(side):
        return pltpu.make_async_remote_copy(
            src_ref=ebuf.at[side], dst_ref=halo.at[1 - side],
            send_sem=edge_send.at[side], recv_sem=edge_recv.at[1 - side],
            device_id={"energy": energy_sides[side][0]}, device_id_type=MESH,
        )

    def slab_copy(side, slot):
        source = xs if slot < raw else own
        landing = (left, right)[side]
        return pltpu.make_async_remote_copy(
            src_ref=source.at[slot], dst_ref=landing.at[slot],
            send_sem=slab_send.at[side, slot], recv_sem=slab_recv.at[side, slot],
            device_id={"atom": sides[side][0]}, device_id_type=MESH,
        )

    def rim_copy(side):
        return pltpu.make_async_remote_copy(
            src_ref=rim, dst_ref=rim_in.at[side],
            send_sem=rim_send.at[side], recv_sem=rim_recv.at[side],
            device_id={"atom": sides[side][0]}, device_id_type=MESH,
        )

    def start_sends(make):
        for side in range(2):

            @pl.when(heard[side])
            def _():
                make(side).start()

    def wait_landed(make, side):
        @pl.when(sides[1 - side][1])
        def _():
            make(side).wait_recv()

    def wait_sent(make):
        for side in range(2):

            @pl.when(sides[side][1])
            def _():
                make(side).wait_send()

    loads[0].wait()
    x32[...] = xv[...].astype(F32).reshape(2 * orb * inner, lanes)
    for slot in range(atoms):
        for r in range(2):
            rows = x32[pl.ds(r * orb * inner + atoms - 1 - slot, pairs, stride=atoms), :]
            xs[slot, r] = rows.astype(BF16)

    pl.semaphore_wait(barrier, expected)
    for slot in range(raw):
        start_sends(functools.partial(slab_copy, slot=slot))

    for side in range(2):

        @pl.when(heard[side])
        def _():
            pl.semaphore_signal(
                answer.at[1 - side], inc=1, device_id={"atom": sides[side][0]}, device_id_type=MESH
            )

    @pl.when(energy_sides[0][1])
    def _():
        pl.semaphore_signal(ready, inc=1, device_id={"energy": energy_sides[0][0]}, device_id_type=MESH)

    split = raw * 2 * pairs
    offset = -(-split // lanes) * lanes
    ebuf[...] = jnp.zeros_like(ebuf)
    flat = [xs[:raw].reshape(split, lanes), xs[raw:].reshape((atoms - raw) * 2 * pairs, lanes)]
    pick_row, pick_col = iota((16, lanes), 0), iota((16, lanes), 1)
    target = jnp.where(pick_row < 8, pick_row - WIDTH, pick_row - 8 + lanes - WIDTH)
    pick = jnp.where((pick_col == target) & (pick_row >= WIDTH) & (pick_row < 12), 1.0, 0.0).astype(BF16)
    edges = [
        lax.dot_general(pick, part, (((1,), (1,)), ((), ())), preferred_element_type=F32).astype(BF16)
        for part in flat
    ]
    for side in range(2):
        ebuf[side, :, :split] = edges[0][side * 8 : side * 8 + 8]
        ebuf[side, :, offset:] = edges[1][side * 8 : side * 8 + 8]

    for side in range(2):

        @pl.when(energy_sides[side][1])
        def _():
            if side == 1:
                pl.semaphore_wait(ready, 1)
            edge_copy(side).start()

    for side, (_, exists) in enumerate(energy_sides):

        @pl.when(jnp.logical_not(exists))
        def _():
            halo[side] = jnp.zeros(halo.shape[1:], BF16)

    for landing, (_, exists) in ((right, sides[0]), (left, sides[1])):

        @pl.when(jnp.logical_not(exists))
        def _():
            landing[...] = jnp.zeros_like(landing)

    for copy in loads[1:4]:
        copy.wait()
    weights = offset_weight_rows(shv[...], stv[...], ocv[...])
    band = band_from_gap(iota((lanes, lanes), 0) - iota((lanes, lanes), 1), weights).astype(BF16)
    edge_row, edge_col = iota((8, lanes), 0), iota((8, lanes), 1)
    edge_energy = jnp.where(edge_row < WIDTH, edge_row - WIDTH, edge_row - WIDTH + lanes)
    corner = band_from_gap(edge_energy - edge_col, weights).astype(BF16)

    def beyond(edge_values):
        return lax.dot_general(edge_values, corner, (((0,), (0,)), ((), ())), preferred_element_type=F32)

    inside = dot(flat[1], band)
    for side in range(2):

        @pl.when(energy_sides[1 - side][1])
        def _():
            edge_copy(side).wait_recv()

    both = [halo[0, :, :split] + halo[1, :, :split], halo[0, :, offset:] + halo[1, :, offset:]]
    rim[...] = both[0]
    start_sends(rim_copy)
    rest = (inside + beyond(both[1])).astype(BF16)
    own[raw:] = rest.reshape(atoms - raw, 2, pairs, lanes)
    for slot in range(raw, atoms):
        start_sends(functools.partial(slab_copy, slot=slot))
    own[:raw] = (dot(flat[0], band) + beyond(both[0])).astype(BF16).reshape(raw, 2, pairs, lanes)

    for atom in range(atoms):
        for o in range(orb):
            values = [
                x32[pl.ds((r * orb + o) * inner + atom, orb, stride=atoms), :] for r in range(2)
            ]
            for part, value in enumerate((values[0], values[1], values[0] + values[1])):
                bpad[atom, part, o, 0:orb, :] = value

    for copy in loads[4:]:
        copy.wait()
    gf[...] = gv[...].astype(F32)
    gz[...] = jnp.zeros_like(gz)
    for atom in range(atoms):
        for bond in range(bonds):
            gz[atom, bond, 0:orb, 0:orb] = gf[pl.ds(bond * inner + atom, orb, stride=atoms), :]
        ga[atom] = gz[atom].reshape(bonds * high, high).astype(BF16)

    reach = 2 * WIDTH
    others = (reach - 1) * pairs
    last = -(-others // lanes) * lanes
    blocks = kbuf.shape[2] // lanes
    table_row = iota((high, lanes), 0)

    def build(step, carry):
        atom, block = step // blocks, lax.rem(step, blocks)
        column = block * lanes + iota((high, lanes), 1)
        early = column < last
        column = jnp.where(early, column, column - last)
        source = column // pairs
        within = column - source * pairs
        k = within // orb
        source = jnp.where(early, source + 1, 0)
        local_id = atom + source + jnp.where(source >= WIDTH, 1, 0)
        spread_k = jnp.where(table_row == k, 1.0, 0.0).astype(BF16)
        spread_l = jnp.where(table_row == within - k * orb, 1.0, 0.0).astype(BF16)
        first_factor = dot(ga[atom], spread_k).reshape(bonds, high, lanes)
        second_factor = dot(ga[atom], spread_l).reshape(bonds, high, lanes)
        for bond in range(bonds):
            hit = local_id == nbs[atom, bond] - here_a * atoms + atoms
            e1[bond] = jnp.where(hit, first_factor[bond], 0.0)
        for o in range(orb):
            total = jnp.zeros((high, lanes), F32)
            for bond in range(bonds):
                total = total + e1[bond, o : o + 1, :] * second_factor[bond]
            kbuf[atom, o * high : (o + 1) * high, pl.ds(pl.multiple_of(block * lanes, lanes), lanes)] = total.astype(BF16)
        return carry

    lax.fori_loop(0, atoms * blocks, build, 0)

    for side in range(2):

        @pl.when(answered[side])
        def _():
            pl.semaphore_wait(answer.at[side], 1)
            for slot in range(raw):
                slab_copy(side, slot).start()
            rim_copy(side).start()
            for slot in range(raw, atoms):
                slab_copy(side, slot).start()

    def phonon(local_id):
        landing = (left, own, right)[local_id // atoms]
        slot = atoms - 1 - local_id % atoms
        return jnp.concatenate([landing[slot, 0], landing[slot, 1]], axis=1)

    def early_sources(atom):
        ids = [atom + step + (1 if step >= WIDTH else 0) for step in range(1, reach)]
        stack = jnp.concatenate([phonon(each) for each in ids], axis=0)
        sacc[...] = dot(kbuf[atom, :, :others], stack)

    tiles = high // 8
    together = 4

    def products(factor, other, row):
        sums = [[jnp.zeros((high, lanes), F32) for _ in range(3)] for _ in range(together)]
        for k in range(orb):
            for part in range(3):
                value = other(part, k)
                for each in range(together):
                    sums[each][part] = sums[each][part] + factor(part, row + each, k) * value
        return [(total[0] - total[1], total[2] - total[0] - total[1]) for total in sums]

    def finish(atom):
        total = sacc[...] + dot(kbuf[atom, :, last : last + pairs], phonon(atom))
        real, imag = total[:, :lanes], total[:, lanes:]
        for part, value in enumerate((real, imag, real + imag)):
            se[part] = value.reshape(orb, high, lanes)

        def first(step, carry):
            row = step * together
            values = products(
                lambda part, i, k: se[part, i, k : k + 1, :], lambda part, k: bpad[atom, part, k], row
            )
            for each, (real, imag) in enumerate(values):
                tbuf[0, row + each] = real
                tbuf[1, row + each] = imag
                tbuf[2, row + each] = real + imag
            return carry

        lax.fori_loop(0, orb // together, first, 0)

        def second(step, carry):
            row = step * together
            values = products(
                lambda part, i, k: bpad[atom, part, i, k : k + 1, :], lambda part, k: tbuf[part, k], row
            )
            for each, parts in enumerate(values):
                for part, value in enumerate(parts):
                    final = (value + bpad[atom, part, row + each])[:orb]
                    out32[pl.ds((part * orb + row + each) * inner + atom, orb, stride=atoms), :] = final
            return carry

        lax.fori_loop(0, orb // together, second, 0)

    def settle_raw(side):
        landing = (left, right)[side]
        for slot in range(raw):
            wait_landed(functools.partial(slab_copy, slot=slot), side)
        wait_landed(rim_copy, side)

        @pl.when(sides[1 - side][1])
        def _():
            sums = (dot(landing[:raw].reshape(split, lanes), band) + beyond(rim_in[side])).astype(BF16)
            landing[:raw] = sums.reshape(raw, 2, pairs, lanes)

    settle_raw(1)
    for slot in range(raw, atoms):
        wait_landed(functools.partial(slab_copy, slot=slot), 1)
    for atom in range(atoms - 1, -1, -1):
        early_sources(atom)
        slot = atoms - 1 - atom
        if slot == 0:
            settle_raw(0)
        elif slot >= raw:
            wait_landed(functools.partial(slab_copy, slot=slot), 0)
        finish(atom)
    out_ref[...] = out32[...].reshape(out_ref.shape).astype(out_ref.dtype)

    for side in range(2):

        @pl.when(energy_sides[side][1])
        def _():
            edge_copy(side).wait_send()

    wait_sent(rim_copy)
    for slot in range(atoms):
        wait_sent(functools.partial(slab_copy, slot=slot))


def per_device(atom_count, energy_count, bare_green, coupling_grad, neighbours, shifts, strength, occupation):
    _, orb, _, atoms, lanes = bare_green.shape
    bonds = coupling_grad.shape[0]
    inner, pairs = orb * atoms, orb * orb
    waves = shifts.shape[0]
    raw = 1
    high = -(-orb // 16) * 16
    x = bare_green.reshape(2, orb, inner, lanes)
    g = jnp.transpose(coupling_grad, (0, 1, 3, 2)).reshape(bonds * inner, orb)
    columns = sum(-(-count * pairs // lanes) * lanes for count in (2 * WIDTH - 1, 1))
    slab = (atoms, 2, pairs, lanes)
    part = raw * 2 * pairs
    rim_columns = -(-part // lanes) * lanes + (atoms - raw) * 2 * pairs
    any_spec = pl.BlockSpec(memory_space=pl.ANY)
    result = pl.pallas_call(
        functools.partial(kernel, orb, bonds, atoms, atom_count, energy_count, raw),
        out_shape=pltpu.VMEM(x.shape, x.dtype),
        in_specs=[any_spec] * 6,
        out_specs=pl.BlockSpec(memory_space=pltpu.VMEM),
        scratch_shapes=[
            pltpu.VMEM(x.shape, BF16),
            pltpu.VMEM(g.shape, BF16),
            pltpu.SMEM(neighbours.shape, jnp.int32),
            pltpu.VMEM((1, waves), jnp.int32),
            pltpu.VMEM((1, waves), F32),
            pltpu.VMEM((1, waves), F32),
            pltpu.VMEM((2 * orb * inner, lanes), F32),
            pltpu.VMEM(slab, BF16),
            pltpu.VMEM((2, 8, rim_columns), BF16),
            pltpu.VMEM((2, 8, rim_columns), BF16),
            pltpu.VMEM((8, part), BF16),
            pltpu.VMEM((2, 8, part), BF16),
            pltpu.VMEM(slab, BF16),
            pltpu.VMEM(slab, BF16),
            pltpu.VMEM(slab, BF16),
            pltpu.VMEM(g.shape, F32),
            pltpu.VMEM((atoms, bonds, high, high), F32),
            pltpu.VMEM((atoms, bonds * high, high), BF16),
            pltpu.VMEM((bonds, high, lanes), F32),
            pltpu.VMEM((atoms, orb * high, columns), BF16),
            pltpu.VMEM((atoms, 3, orb, high, lanes), F32),
            pltpu.VMEM((orb * high, 2 * lanes), F32),
            pltpu.VMEM((3, orb, high, lanes), F32),
            pltpu.VMEM((3, orb, high, lanes), F32),
            pltpu.VMEM((2 * orb * inner, lanes), F32),
            pltpu.SemaphoreType.REGULAR,
            pltpu.SemaphoreType.REGULAR((2,)),
            pltpu.SemaphoreType.DMA((6,)),
            pltpu.SemaphoreType.DMA((2,)),
            pltpu.SemaphoreType.DMA((2,)),
            pltpu.SemaphoreType.DMA((2,)),
            pltpu.SemaphoreType.DMA((2,)),
            pltpu.SemaphoreType.DMA((2, atoms)),
            pltpu.SemaphoreType.DMA((2, atoms)),
        ],
        compiler_params=pltpu.CompilerParams(collective_id=0, has_side_effects=True),
    )(x, g, neighbours, shifts.reshape(1, waves), strength.reshape(1, waves), occupation.reshape(1, waves))
    return result.reshape(bare_green.shape)


def solution(mesh):
    placed = (
        P(None, None, None, "atom", "energy"),
        P(None, None, None, "atom"),
        P("atom", None),
        P(),
        P(),
        P(),
    )
    body = functools.partial(per_device, mesh.shape["atom"], mesh.shape["energy"])
    return jax.shard_map(
        body,
        mesh=mesh,
        in_specs=placed,
        out_specs=P(None, None, None, "atom", "energy"),
        check_vma=False,
    )
```

time: 109 us -> 36 us (0.33)
  the two profiles are of different devices: /device:TPU:57 before, /device:TPU:1 now
where the time goes in v2:
time: 36 us; the launch traced here: 35.8 us
  Pallas kernels  35.1 us (98%)
  local copies, waits for them, and re-layouts  0.72 us (2%)
    pallas_call x1, Pallas kernels, per_device(): pl.pallas_call(functools.partial(kernel, orb, bonds, atoms, atom_count, e...  35.1 us

profile of v2, /device:TPU:1, one launch (start us, length us, event | category | flops | bytes accessed | tf_op | source)
XLA Modules:
  0.0 35.8 jit_solution(13673153954595921378)
XLA Ops:
  0.0 35.1 %shard_map.64 = bf16[2,12,48,128]{3,2,1,0:T(8,128)(2,1)S(1)} custom-call(bf16[2,12,48,128]{3,2,1,0:T(8,128)(2,1)} %bitcast.9, bf16[384,12]{1,0:T(8,128)(2,1)} %bitcast.10, s32[4,8]{1,0:T(4,128)} %nb_hbm.1, s32[1,32]{1,0:T(1,128)} %bitcast.11, f32[1,32]{1,0:T(1,128)} %bitcast.12, f32[1,32]{1,0:T(1,128)} %bitcast.13), custom_call_target="tpu_custom_call" | custom-call | tf_op jit(solution)/shard_map/pallas_call | solution.py:376
  35.1 0.7 %copy.8 = bf16[2,12,12,4,128]{4,3,2,1,0:T(4,128)(2,1)} copy(bf16[2,12,12,4,128]{4,3,2,1,0:T(4,128)(2,1)S(1)} %bitcast.8) | data formatting | bytes 589824

commit v3 on v2

--- a/solution.py
+++ b/solution.py
@@ -206,8 +206,13 @@
     start_sends(rim_copy)
     rest = (inside + beyond(both[1])).astype(BF16)
     own[raw:] = rest.reshape(atoms - raw, 2, pairs, lanes)
-    for slot in range(raw, atoms):
-        start_sends(functools.partial(slab_copy, slot=slot))
+    for order in zip(range(raw, atoms), reversed(range(raw, atoms))):
+        for side in range(2):
+
+            @pl.when(heard[side])
+            def _():
+                slab_copy(side, order[side]).start()
+
     own[:raw] = (dot(flat[0], band) + beyond(both[0])).astype(BF16).reshape(raw, 2, pairs, lanes)
 
     for atom in range(atoms):
@@ -267,7 +272,7 @@
             for slot in range(raw):
                 slab_copy(side, slot).start()
             rim_copy(side).start()
-            for slot in range(raw, atoms):
+            for slot in range(raw, atoms) if side == 0 else reversed(range(raw, atoms)):
                 slab_copy(side, slot).start()
 
     def phonon(local_id):
@@ -336,16 +341,29 @@
             landing[:raw] = sums.reshape(raw, 2, pairs, lanes)
 
     settle_raw(1)
-    for slot in range(raw, atoms):
-        wait_landed(functools.partial(slab_copy, slot=slot), 1)
-    for atom in range(atoms - 1, -1, -1):
-        early_sources(atom)
-        slot = atoms - 1 - atom
-        if slot == 0:
-            settle_raw(0)
-        elif slot >= raw:
-            wait_landed(functools.partial(slab_copy, slot=slot), 0)
-        finish(atom)
+
+    @pl.when(here_a == 0)
+    def _():
+        for atom in range(atoms):
+            slot = atoms - 1 - atom
+            if slot >= raw:
+                wait_landed(functools.partial(slab_copy, slot=slot), 1)
+            early_sources(atom)
+            finish(atom)
+
+    @pl.when(here_a > 0)
+    def _():
+        for slot in reversed(range(raw, atoms)):
+            wait_landed(functools.partial(slab_copy, slot=slot), 1)
+        for atom in range(atoms - 1, -1, -1):
+            early_sources(atom)
+            slot = atoms - 1 - atom
+            if slot == 0:
+                settle_raw(0)
+            elif slot >= raw:
+                wait_landed(functools.partial(slab_copy, slot=slot), 0)
+            finish(atom)
+
     out_ref[...] = out32[...].reshape(out_ref.shape).astype(out_ref.dtype)
 
     for side in range(2):

time: 36 us -> 33.7 us (0.936)
  Pallas kernels: 35.1 us -> 32.8 us
    pallas_call x1, Pallas kernels: 35.1 us -> 32.8 us  [per_device(): pl.pallas_call(functools.partial(kernel, orb, bonds, atoms, atom_count, e...]
where the time goes in v3:
time: 33.7 us; the launch traced here: 33.6 us
  Pallas kernels  32.8 us (97%)
  local copies, waits for them, and re-layouts  0.72 us (2%)
    pallas_call x1, Pallas kernels, per_device(): pl.pallas_call(functools.partial(kernel, orb, bonds, atoms, atom_count, e...  32.8 us
    unnamed x1, local copies, waits for them, and re-layouts  0.72 us

profile of v3, /device:TPU:1, one launch (start us, length us, event | category | flops | bytes accessed | tf_op | source)
XLA Modules:
  0.0 33.6 jit_solution(6605258880915906362)
XLA Ops:
  0.0 32.8 %shard_map.64 = bf16[2,12,48,128]{3,2,1,0:T(8,128)(2,1)S(1)} custom-call(bf16[2,12,48,128]{3,2,1,0:T(8,128)(2,1)} %bitcast.9, bf16[384,12]{1,0:T(8,128)(2,1)} %bitcast.10, s32[4,8]{1,0:T(4,128)} %nb_hbm.1, s32[1,32]{1,0:T(1,128)} %bitcast.11, f32[1,32]{1,0:T(1,128)} %bitcast.12, f32[1,32]{1,0:T(1,128)} %bitcast.13), custom_call_target="tpu_custom_call" | custom-call | tf_op jit(solution)/shard_map/pallas_call | solution.py:394
  32.8 0.7 %copy.8 = bf16[2,12,12,4,128]{4,3,2,1,0:T(4,128)(2,1)} copy(bf16[2,12,12,4,128]{4,3,2,1,0:T(4,128)(2,1)S(1)} %bitcast.8) | data formatting | bytes 589824
